TPU v7x, 256 devices: a whole 4x4x8 slice. The times are simulated.
256 devices in a mesh: dp: 8 (over x, y_hi), ctx: 32 (over y_lo, z, core).
Axes of the slice: x: 4, y: 4 (y_hi: 2, y_lo: 2; y = y_hi * 2 + y_lo), z: 8, core: 2. Of those that a mesh axis runs over, the one named last changes fastest.
Arguments:
- projections: bfloat16 [3072, 65536], P(None, ('dp', 'ctx')), may hold values from -6 to 6
- short_filter: bfloat16 [7, 3072], replicated, may hold values from -2 to 2
- long_filter: bfloat16 [256, 65536], P(('dp', 'ctx')), may hold values from -6 to 6
- out_grad: bfloat16 [1024, 65536], P(None, ('dp', 'ctx')), may hold values from -3 to 3
Outputs:
- mixed: bfloat16 [1024, 65536], P(None, ('dp', 'ctx'))
- proj_grad: bfloat16 [3072, 65536], P(None, ('dp', 'ctx'))
- filter_grad: float32 [256, 65536], P(('dp', 'ctx'))
All inputs are finite; a program needn't handle non-finite values.
Results may differ from a plain program's by a relative error of at most 0.01.
Values may be sent and summed in bfloat16 or wider, within the bound.
A program may use at most 64 MiB of HBM per device.

v0:
```python
import functools
import math

import jax
import jax.numpy as jnp
import numpy as np
from jax import lax
from jax.experimental import pallas as pl
from jax.experimental.pallas import tpu as pltpu
from jax.sharding import PartitionSpec as P

CPG = 4
TAPS = 7
LANES = 32
CH = 1024
SEQ = 65536
PAD = 2 * SEQ
A = 256
B = 512
HALF = 256
ROWS = 272
CHIPS = 128
DEVICES = 256
SCALE = SEQ ** -0.5
BLOCK = 512
NT = (((1,), (1,)), ((), ()))
TN = (((0,), (0,)), ((), ()))
F32 = jnp.float32
BF16 = jnp.bfloat16


def make_tables():
    order = np.concatenate([np.arange(0, HALF, 2), np.arange(1, HALF, 2)])
    d = np.arange(HALF)[:, None]
    outer = 2 * np.pi * ((d * order[None, :]) % B) / B
    cos_outer, sin_outer = np.cos(outer), np.sin(outer)
    sign = 1.0 - 2.0 * (order % 2)
    spread = np.zeros((2 * HALF + 16, HALF))
    spread[:HALF] = cos_outer
    spread[HALF : 2 * HALF] = -sin_outer
    spread[2 * HALF] = sign
    gather = np.zeros((HALF, 2 * HALF))
    gather[:, :HALF] = 2 * cos_outer.T
    gather[:, 0] = 1.0
    gather[:, HALF:] = -2 * sin_outer.T
    gather[:, HALF] = sign
    e = np.arange(A)
    inner = 2 * np.pi * ((e[:, None] * e[None, :]) % A) / A
    cos_inner, sin_inner = np.cos(inner), np.sin(inner)
    mix = np.block([[cos_inner, -sin_inner], [sin_inner, cos_inner]])
    twist = 2 * np.pi * (np.arange(ROWS)[:, None] * e[None, :]) / PAD
    return (
        jnp.asarray(spread.astype(np.float32), BF16),
        jnp.asarray(gather.astype(np.float32), BF16),
        jnp.asarray(mix.astype(np.float32), BF16),
        jnp.asarray(np.cos(twist).astype(np.float32)),
        jnp.asarray(np.sin(twist).astype(np.float32)),
    )


def place(index):
    return (index // LANES, index % LANES)


def signal(sem, index):
    pl.semaphore_signal(sem, inc=1, device_id=place(index), device_id_type=pl.DeviceIdType.MESH)


def remote(source, target, sems, index):
    return pltpu.make_async_remote_copy(
        source, target, sems.at[0], sems.at[1], device_id=place(index), device_id_type=pl.DeviceIdType.MESH
    )


def dot(first, second):
    return jnp.dot(first, second, preferred_element_type=F32)


def one_hot(shape, offset, limit):
    row = lax.broadcasted_iota(jnp.int32, shape, 0)
    lane = lax.broadcasted_iota(jnp.int32, shape, 1)
    return ((lane == row + offset) & (row < limit)).astype(F32).astype(BF16)


def mixer_kernel(
    proj, taps, filt, grad, spread, gather, mix, cos_twist, sin_twist,
    mixed, pgrad, fgrad,
    weights, shift, feat, prod, cotp, recv_p, recv_g, fold, signals, swap_out, swap_in, kept, ready_c, ready_b, tok_c, tok_b,
    fspec, kspec, cross, bins, rows, mixback, dfeat, edge_out, edge_in, edge_q,
    rounds, sem_edge, sem_edge_q, sem_edge_kv, sem_p, sem_g, sem_c, sem_b, swap_p, swap_g, swap_c, swap_b, own,
):
    me = lax.axis_index("dp") * LANES + lax.axis_index("ctx")
    chip, core = me // 2, me % 2
    high, low = me // 16, me % 16
    twin = chip * 2 + 1 - core
    after, before = (me + 1) % DEVICES, (me + DEVICES - 1) % DEVICES
    mine = pl.ds(pl.multiple_of(core * CHIPS, CHIPS), CHIPS)
    theirs = pl.ds(pl.multiple_of((1 - core) * CHIPS, CHIPS), CHIPS)

    gate = pltpu.get_barrier_semaphore()
    for step in range(1, 16):
        signal(gate, high * 16 + (low + step) % 16)
    for step in range(1, 16):
        signal(gate, ((high + step) % 16) * 16 + low)
    signal(gate, after)
    signal(gate, before)

    last = one_hot((16, A), A - TAPS + 1, TAPS - 1)
    first = one_hot((16, A), 0, TAPS - 1)
    for block in range(0, 3 * CH, BLOCK):
        edge_out[0, :, block : block + BLOCK] = lax.dot_general(
            last, proj[block : block + BLOCK, :], NT, preferred_element_type=F32
        ).astype(BF16)
    for block in range(0, 3 * CH, 128):
        weights[block : block + 128, :] = jnp.transpose(taps[:, block : block + 128])
    row = lax.broadcasted_iota(jnp.int32, (A, 128), 0)
    lane = lax.broadcasted_iota(jnp.int32, (A, 128), 1)
    for lag in range(1, TAPS):
        span = slice((lag - 1) * 128, lag * 128)
        shift[0, :, span] = (row == lane + 128 - lag).astype(F32).astype(BF16)
        shift[1, :, span] = (row == lane + lag).astype(F32).astype(BF16)
    mixback[:A, :A] = mix[:A, :A]
    mixback[A:, A:] = mix[A:, A:]
    mixback[:A, A:] = mix[A:, :A]
    mixback[A:, :A] = mix[:A, A:]

    def forward(signal_rows):
        raw = dot(spread[...], signal_rows)
        re, im, odd = raw[:HALF], raw[HALF : 2 * HALF], raw[2 * HALF :]
        ct, st = cos_twist[:HALF, :], sin_twist[:HALF, :]
        bins[:HALF, :A] = (re * ct + im * st).astype(BF16)
        bins[:HALF, A:] = (im * ct - re * st).astype(BF16)
        bins[HALF:, :A] = (odd * cos_twist[HALF:, :]).astype(BF16)
        bins[HALF:, A:] = (-odd * sin_twist[HALF:, :]).astype(BF16)
        return dot(bins[...], mix[...])

    def inverse(re, im):
        bins[:, :A] = re.astype(BF16)
        bins[:, A:] = im.astype(BF16)
        back = dot(bins[...], mixback[...])
        re, im = back[:, :A], back[:, A:]
        ct, st = cos_twist[...], sin_twist[...]
        turn_re = re * ct - im * st
        turn_im = im[:HALF] * ct[:HALF] + re[:HALF] * st[:HALF]
        top = lax.broadcasted_iota(jnp.int32, (16, A), 0) == 0
        rows[:HALF, :] = turn_re[:HALF].astype(BF16)
        rows[HALF:, :] = turn_im.astype(BF16)
        rows[HALF : HALF + 16, :] = jnp.where(top, turn_re[HALF:], turn_im[:16]).astype(BF16)
        return dot(gather[...], rows[...]) * (1.0 / PAD)

    pl.semaphore_wait(gate, 32)
    edge = remote(edge_out.at[0], edge_in.at[0], sem_edge, after)
    edge.start()
    for step in range(1, 16):
        signal(rounds.at[0], high * 16 + (low + step) % 16)

    for half in range(2):
        lanes = slice(half * 128, half * 128 + 128)
        fold[half, :HALF, :] = filt[:, lanes].astype(F32)
        for parity in range(2):
            rows[parity * CHIPS : (parity + 1) * CHIPS, lanes] = fold[
                half, pl.ds(parity, CHIPS, stride=2), :
            ].astype(BF16)
    fspec[...] = forward(rows[:HALF, :])

    pl.semaphore_wait(rounds.at[0], 15)
    for step in range(1, 16):
        signal(rounds.at[1], ((high + step) % 16) * 16 + low)

    edge.wait()
    ahead = one_hot((16, 128), 128 - TAPS + 1, TAPS - 1)
    behind = one_hot((16, 128), 0, TAPS - 1)

    def filtered(start):
        span = pl.ds(pl.multiple_of(start, BLOCK), BLOCK)
        prior = lax.dot_general(edge_in[0, :, span], ahead, TN, preferred_element_type=F32).astype(BF16)
        prior = jnp.where(me > 0, prior, jnp.zeros_like(prior))
        block = proj[span, :]
        scale = weights[span, :]
        halves = []
        for half, window in ((0, jnp.concatenate([prior, block[:, :128]], axis=1)), (1, block)):
            moved = dot(window, shift[0])
            total = scale[:, 0:1] * block[:, half * 128 : half * 128 + 128].astype(F32)
            for lag in range(1, TAPS):
                total = total + scale[:, lag : lag + 1] * moved[:, (lag - 1) * 128 : lag * 128]
            total = total.astype(BF16)
            feat[span, half * 128 : half * 128 + 128] = total
            halves.append(total.astype(F32))
        return halves

    def make_product(step, carry):
        keys = filtered(CH + step * BLOCK)
        values = filtered(2 * CH + step * BLOCK)
        for half in range(2):
            both = (keys[half] * values[half]).reshape(BLOCK // 8, 8, 128)
            prod[pl.ds(step * (BLOCK // 8), BLOCK // 8), :, half * 128 : half * 128 + 128] = both.astype(BF16)
        return carry

    def make_cotangent(step, carry):
        queries = filtered(step * BLOCK)
        span = pl.ds(pl.multiple_of(step * BLOCK, BLOCK), BLOCK)
        for half in range(2):
            lanes = slice(half * 128, half * 128 + 128)
            both = (queries[half] * grad[span, lanes].astype(F32)).reshape(BLOCK // 8, 8, 128)
            cotp[pl.ds(step * (BLOCK // 8), BLOCK // 8), :, lanes] = both.astype(BF16)
        return carry

    def send_all(source, target, sems, slot):
        def send(step, carry):
            other = (chip + step) % CHIPS
            remote(source.at[other], target.at[chip], sems, other * 2 + core).start()
            return carry

        lax.fori_loop(1, CHIPS, send, 0)
        keep = pltpu.make_async_copy(source.at[chip], target.at[chip], own.at[slot])
        keep.start()
        return keep

    def settle(source, target, sems, keep):
        keep.wait()
        others = pl.ds(0, CHIPS - 1)
        whole = remote(source.at[others], target.at[others], sems, ((chip + 1) % CHIPS) * 2 + core)
        whole.wait_send()
        whole.wait_recv()

    lax.fori_loop(0, CH // BLOCK, make_product, 0)
    pl.semaphore_wait(rounds.at[1], 15)
    keep_p = send_all(prod, recv_p, sem_p, 0)
    lax.fori_loop(0, CH // BLOCK, make_cotangent, 0)
    keep_g = send_all(cotp, recv_g, sem_g, 1)

    def unfold(received, stream, swap):
        for half in range(2):
            lanes = slice(half * 128, half * 128 + 128)
            fold[half] = received[:, :, lanes].astype(F32).reshape(CHIPS * 8, 128)
            for channel in range(CPG):
                low_set = fold[half, pl.ds(channel, CHIPS, stride=8), :]
                high_set = fold[half, pl.ds(CPG + channel, CHIPS, stride=8), :]
                signals[stream * CPG + channel, mine, lanes] = jnp.where(core == 0, low_set, high_set).astype(BF16)
                swap_out[stream, channel, :, lanes] = jnp.where(core == 0, high_set, low_set).astype(BF16)
        moved = remote(
            swap_out.at[stream], signals.at[pl.ds(stream * CPG, CPG), mine, :], swap, twin
        )
        moved.start()
        moved.wait()

    def refold(stream, ready, swap):
        moved = remote(swap_out.at[2 + stream], swap_in.at[stream], swap, twin)
        moved.start()
        moved.wait()
        for half in range(2):
            lanes = slice(half * 128, half * 128 + 128)
            for channel in range(CPG):
                here = kept[stream, channel, :, lanes].astype(F32)
                there = swap_in[stream, channel, :, lanes].astype(F32)
                fold[half, pl.ds(channel, CHIPS, stride=8), :] = jnp.where(core == 0, here, there)
                fold[half, pl.ds(CPG + channel, CHIPS, stride=8), :] = jnp.where(core == 0, there, here)
            ready[:, :, lanes] = fold[half].reshape(CHIPS, 8, 128).astype(BF16)

    def put_away(result, stream, channel):
        even, odd = result[:CHIPS], result[CHIPS:]
        kept[stream, channel] = jnp.where(core == 0, even, odd).astype(BF16)
        swap_out[2 + stream, channel] = jnp.where(core == 0, odd, even).astype(BF16)

    settle(prod, recv_p, sem_p, keep_p)
    unfold(recv_p, 0, swap_p)

    def convolve(channel, carry):
        spec = forward(signals[channel])
        kspec[channel] = spec
        re, im = spec[:, :A], spec[:, A:]
        f_re, f_im = fspec[:, :A], fspec[:, A:]
        put_away(inverse((f_re * re - f_im * im) * SCALE, (f_re * im + f_im * re) * SCALE), 0, channel)
        return carry

    lax.fori_loop(0, CPG, convolve, 0)
    refold(0, ready_c, swap_c)
    keep_c = send_all(ready_c, tok_c, sem_c, 2)

    settle(cotp, recv_g, sem_g, keep_g)
    unfold(recv_g, 1, swap_g)
    cross[...] = jnp.zeros_like(cross)

    def correlate(channel, carry):
        spec = forward(signals[CPG + channel])
        re, im = spec[:, :A], spec[:, A:]
        k_re, k_im = kspec[channel, :, :A], kspec[channel, :, A:]
        cross[:, :A] = cross[:, :A] + (k_re * re + k_im * im)
        cross[:, A:] = cross[:, A:] + (k_re * im - k_im * re)
        f_re, f_im = fspec[:, :A], fspec[:, A:]
        put_away(inverse((f_re * re + f_im * im) * SCALE, (f_re * im - f_im * re) * SCALE), 1, channel)
        return carry

    lax.fori_loop(0, CPG, correlate, 0)
    refold(1, ready_b, swap_b)
    keep_b = send_all(ready_b, tok_b, sem_b, 3)

    result = inverse(cross[:, :A], cross[:, A:]) * SCALE
    for parity in range(2):
        for half in range(2):
            fold[half, pl.ds(parity, CHIPS, stride=2), :] = result[
                parity * CHIPS : (parity + 1) * CHIPS, half * 128 : half * 128 + 128
            ]
    for half in range(2):
        fgrad[:, half * 128 : half * 128 + 128] = fold[half, :HALF, :]

    settle(ready_c, tok_c, sem_c, keep_c)

    def use_conv(step, carry):
        span = pl.ds(pl.multiple_of(step * BLOCK, BLOCK), BLOCK)
        conv = tok_c[pl.ds(step * (BLOCK // 8), BLOCK // 8)].astype(F32).reshape(BLOCK, A)
        mixed[span, :] = (feat[span, :].astype(F32) * conv).astype(BF16)
        back = (grad[span, :].astype(F32) * conv).astype(BF16)
        dfeat[span, :] = back
        edge_q[0, :, span] = lax.dot_general(first, back, NT, preferred_element_type=F32).astype(BF16)
        return carry

    lax.fori_loop(0, CH // BLOCK, use_conv, 0)
    edge_back = remote(edge_q.at[0], edge_q.at[1], sem_edge_q, before)
    edge_back.start()
    edge_back.wait()

    def gathered(start, halo):
        span = pl.ds(pl.multiple_of(start, BLOCK), BLOCK)
        later = lax.dot_general(halo, behind, TN, preferred_element_type=F32).astype(BF16)
        later = jnp.where(me < DEVICES - 1, later, jnp.zeros_like(later))
        block = dfeat[span, :]
        scale = weights[span, :]
        for half, window in ((0, block), (1, jnp.concatenate([block[:, 128:], later], axis=1))):
            lanes = slice(half * 128, half * 128 + 128)
            moved = dot(window, shift[1])
            total = scale[:, 0:1] * block[:, lanes].astype(F32)
            for lag in range(1, TAPS):
                total = total + scale[:, lag : lag + 1] * moved[:, (lag - 1) * 128 : lag * 128]
            pgrad[span, lanes] = total.astype(BF16)

    def finish_query(step, carry):
        gathered(step * BLOCK, edge_q[1, :, pl.ds(pl.multiple_of(step * BLOCK, BLOCK), BLOCK)])
        return carry

    lax.fori_loop(0, CH // BLOCK, finish_query, 0)
    settle(ready_b, tok_b, sem_b, keep_b)

    def use_back(step, carry):
        back = tok_b[pl.ds(step * (BLOCK // 8), BLOCK // 8)].astype(F32).reshape(BLOCK, A)
        for part, other in ((1, 2), (2, 1)):
            source = pl.ds(pl.multiple_of(other * CH + step * BLOCK, BLOCK), BLOCK)
            target = pl.ds(pl.multiple_of(part * CH + step * BLOCK, BLOCK), BLOCK)
            result = (feat[source, :].astype(F32) * back).astype(BF16)
            dfeat[target, :] = result
            edge_out[1, :, target] = lax.dot_general(first, result, NT, preferred_element_type=F32).astype(BF16)
        return carry

    lax.fori_loop(0, CH // BLOCK, use_back, 0)
    tail = pl.ds(CH, 2 * CH)
    edge_last = remote(edge_out.at[1, :, tail], edge_in.at[1, :, tail], sem_edge_kv, before)
    edge_last.start()
    edge_last.wait()

    def finish_rest(step, carry):
        gathered(CH + step * BLOCK, edge_in[1, :, pl.ds(pl.multiple_of(CH + step * BLOCK, BLOCK), BLOCK)])
        return carry

    lax.fori_loop(0, 2 * CH // BLOCK, finish_rest, 0)


def shards(projections, short_filter, long_filter, out_grad):
    taps = jnp.pad(short_filter.astype(F32), ((0, 8 - TAPS), (0, 0)))
    vmem = pl.BlockSpec(memory_space=pltpu.VMEM)
    tokens = pltpu.VMEM((CHIPS, 8, A), BF16)
    pair = pltpu.SemaphoreType.DMA((2,))
    mixed, proj_grad, filter_grad = pl.pallas_call(
        mixer_kernel,
        out_shape=(
            jax.ShapeDtypeStruct((CH, A), BF16),
            jax.ShapeDtypeStruct((3 * CH, A), BF16),
            jax.ShapeDtypeStruct((HALF, A), F32),
        ),
        in_specs=[vmem] * 9,
        out_specs=(vmem, vmem, vmem),
        scratch_shapes=[
            pltpu.VMEM((3 * CH, 8), F32),
            pltpu.VMEM((2, A, 128 * (TAPS - 1)), BF16),
            pltpu.VMEM((3 * CH, A), BF16),
            tokens, tokens, tokens, tokens,
            pltpu.VMEM((2, CHIPS * 8, 128), F32),
            pltpu.VMEM((2 * CPG, HALF, A), BF16),
            pltpu.VMEM((4, CPG, CHIPS, A), BF16),
            pltpu.VMEM((2, CPG, CHIPS, A), BF16),
            pltpu.VMEM((2, CPG, CHIPS, A), BF16),
            tokens, tokens, tokens, tokens,
            pltpu.VMEM((ROWS, 2 * A), F32),
            pltpu.VMEM((CPG, ROWS, 2 * A), F32),
            pltpu.VMEM((ROWS, 2 * A), F32),
            pltpu.VMEM((ROWS, 2 * A), BF16),
            pltpu.VMEM((2 * HALF, A), BF16),
            pltpu.VMEM((2 * A, 2 * A), BF16),
            pltpu.VMEM((3 * CH, A), BF16),
            pltpu.VMEM((2, 16, 3 * CH), BF16),
            pltpu.VMEM((2, 16, 3 * CH), BF16),
            pltpu.VMEM((2, 16, CH), BF16),
            pltpu.SemaphoreType.REGULAR((2,)),
            pair, pair, pair, pair, pair, pair, pair, pair, pair, pair, pair,
            pltpu.SemaphoreType.DMA((4,)),
        ],
        compiler_params=pltpu.CompilerParams(collective_id=0, has_side_effects=True, vmem_limit_bytes=60 << 20),
        name="mixer",
    )(projections, taps, long_filter.reshape(HALF, A), out_grad, *make_tables())
    return (mixed, proj_grad, filter_grad.reshape(1, SEQ))


def solution(mesh):
    placed = (P(None, ("dp", "ctx")), P(), P(("dp", "ctx"), None), P(None, ("dp", "ctx")))
    return jax.shard_map(
        shards,
        mesh=mesh,
        in_specs=placed,
        out_specs=(P(None, ("dp", "ctx")), P(None, ("dp", "ctx")), P(("dp", "ctx"), None)),
        check_vma=False,
    )
```

profile of v0, /device:TPU:1, one launch (start us, length us, event | category | flops | bytes accessed | tf_op | source)
XLA Modules:
  0.0 87.0 jit_solution(17896856517582010257)
XLA Ops:
  0.6 1.4 %pad_convert_fusion.taps = f32[8,3072]{1,0:T(8,128)} fusion(bf16[7,3072]{1,0:T(8,128)(2,1)} %param.10), kind=kLoop, calls=%fused_computation | loop fusion | flops 24576 | bytes 141312 | tf_op jit(solution)/shard_map/jit(_pad)/pad | solution.py:368
  2.1 1.7 %reduce = bf16[65536]{0:T(1024)(128)(2,1)S(1)} reduce(bf16[1,65536]{1,0:T(2,128)(2,1)} %param.11, bf16[]{:T(256)} %constant.22), dimensions={0}, to_apply=%param.11.reduce_sub_computation | reduce | bytes 262146 | tf_op args[2]
  3.8 0.7 reshape.12.filt
  4.5 77.5 %mixer.1 = (bf16[1024,256]{1,0:T(8,128)(2,1)}, bf16[3072,256]{1,0:T(8,128)(2,1)}, f32[256,256]{1,0:T(8,128)}) custom-call(bf16[3072,256]{1,0:T(8,128)(2,1)} %proj.1, f32[8,3072]{1,0:T(8,128)} %pad_convert_fusion.taps, bf16[256,256]{1,0:T(8,128)(2,1)} %reshape.12.filt, bf16[1024,256]{1,0:T(8,128)(2,1)} %grad.1, bf16[528,256]{1,0:T(8,128)(2,1)} %constant.14.clone.spread, ...), custom_call_target="tpu_custom_call" | custom-call | tf_op jit(solution)/shard_map/mixer/pallas_call | solution.py:372
  81.9 0.0 copy-start
  81.9 2.0 %copy.12 = f32[1,1,256,256]{3,1,2,0:T(1,128)} copy(f32[1,1,256,256]{3,2,1,0:T(8,128)} %bitcast.3) | data formatting | bytes 524288
  84.0 1.9 %copy.15 = bf16[1024,256]{1,0:T(8,128)(2,1)} copy(bf16[1024,256]{1,0:T(8,128)(2,1)} %get-tuple-element.12) | data formatting | bytes 1048576
  85.8 0.0 copy-done
  85.9 1.1 %copy.16 = bf16[3072,256]{1,0:T(8,128)(2,1)} copy(bf16[3072,256]{1,0:T(8,128)(2,1)S(1)} %copy-done) | data formatting | bytes 3145728
Async XLA Ops:
  81.9 3.9 %copy-start = (bf16[3072,256]{1,0:T(8,128)(2,1)S(1)}, bf16[3072,256]{1,0:T(8,128)(2,1)}, u32[]{:S(2)}) copy-start(bf16[3072,256]{1,0:T(8,128)(2,1)} %get-tuple-element.13) | copy-start | bytes 4718596
where the time goes:
time: 87.2 us; the launch traced here: 87 us
  Pallas kernels  77.5 us (89%)
  local copies, waits for them, and re-layouts  5.76 us (7%)
  other arithmetic  3.12 us (4%)
    pallas_call x1, Pallas kernels, shards(): pl.pallas_call(mixer_kernel, out_shape=(jax.ShapeDtypeStruct((CH, A), BF1...  77.5 us
    unnamed x5, local copies, waits for them, and re-layouts  5.05 us

commit v1 on v0

v1 whole, which is shorter than its diff:
```python
import functools
import math

import jax
import jax.numpy as jnp
import numpy as np
from jax import lax
from jax.experimental import pallas as pl
from jax.experimental.pallas import tpu as pltpu
from jax.sharding import PartitionSpec as P

CPG = 4
TAPS = 7
LANES = 32
CH = 1024
SEQ = 65536
PAD = 2 * SEQ
A = 256
B = 512
HALF = 256
ROWS = 272
CHIPS = 128
DEVICES = 256
SCALE = SEQ ** -0.5
BLOCK = 512
SIDE = 64
NT = (((1,), (1,)), ((), ()))
TN = (((0,), (0,)), ((), ()))
F32 = jnp.float32
BF16 = jnp.bfloat16


def make_tables():
    order = np.concatenate([np.arange(0, HALF, 2), np.arange(1, HALF, 2)])
    d = np.arange(HALF)[:, None]
    outer = 2 * np.pi * ((d * order[None, :]) % B) / B
    cos_outer, sin_outer = np.cos(outer), np.sin(outer)
    sign = 1.0 - 2.0 * (order % 2)
    spread = np.zeros((2 * HALF + 16, HALF))
    spread[:HALF] = cos_outer
    spread[HALF : 2 * HALF] = -sin_outer
    spread[2 * HALF] = sign
    gather = np.zeros((HALF, 2 * HALF))
    gather[:, :HALF] = 2 * cos_outer.T
    gather[:, 0] = 1.0
    gather[:, HALF:] = -2 * sin_outer.T
    gather[:, HALF] = sign
    e = np.arange(A)
    inner = 2 * np.pi * ((e[:, None] * e[None, :]) % A) / A
    cos_inner, sin_inner = np.cos(inner), np.sin(inner)
    mix = np.block([[cos_inner, -sin_inner], [sin_inner, cos_inner]])
    twist = 2 * np.pi * (np.arange(ROWS)[:, None] * e[None, :]) / PAD
    return (
        jnp.asarray(spread.astype(np.float32), BF16),
        jnp.asarray(gather.astype(np.float32), BF16),
        jnp.asarray(mix.astype(np.float32), BF16),
        jnp.asarray(np.cos(twist).astype(np.float32)),
        jnp.asarray(np.sin(twist).astype(np.float32)),
    )


def place(index):
    return (index // LANES, index % LANES)


def signal(sem, index):
    pl.semaphore_signal(sem, inc=1, device_id=place(index), device_id_type=pl.DeviceIdType.MESH)


def remote(source, target, sems, index):
    return pltpu.make_async_remote_copy(
        source, target, sems.at[0], sems.at[1], device_id=place(index), device_id_type=pl.DeviceIdType.MESH
    )


def dot(first, second):
    return jnp.dot(first, second, preferred_element_type=F32)


def one_hot(shape, offset, limit):
    row = lax.broadcasted_iota(jnp.int32, shape, 0)
    lane = lax.broadcasted_iota(jnp.int32, shape, 1)
    return ((lane == row + offset) & (row < limit)).astype(F32).astype(BF16)


def mixer_kernel(
    proj_hbm, taps_hbm, filt_hbm, grad_hbm, spread_hbm, gather_hbm, mix_hbm, cos_hbm, sin_hbm,
    mixed, pgrad, fgrad,
    proj, taps, filt, grad, spread, gather, mix, cos_twist, sin_twist, padded,
    weights, shift, feat, prod, cotp, recv_p, recv_g, fold, signals, swap_out, swap_in, kept, ready_c, ready_b, tok_c, tok_b,
    fspec, kspec, cross, bins, rows, mixback, dfeat, edge_out, edge_in, edge_q,
    rounds, loads, sem_edge, sem_edge_q, sem_edge_own, sem_edge_rest, sem_first, sem_p, sem_g, sem_c, sem_b,
    swap_p, swap_g, swap_c, swap_b, own,
):
    me = lax.axis_index("dp") * LANES + lax.axis_index("ctx")
    chip, core = me // 2, me % 2
    high, low = me // 16, me % 16
    side, within = chip // SIDE, chip % SIDE
    twin = chip * 2 + 1 - core
    after, before = (me + 1) % DEVICES, (me + DEVICES - 1) % DEVICES
    mine = pl.ds(pl.multiple_of(core * CHIPS, CHIPS), CHIPS)

    def channels(part, turn):
        return pl.multiple_of(part * CH + (side * (1 - turn) + (1 - side) * turn) * BLOCK, BLOCK)

    def load(source, target, slot):
        copy = pltpu.make_async_copy(source, target, loads.at[slot])
        copy.start()
        return copy

    taps_load = load(taps_hbm, taps, 0)
    parts = {}
    for slot, (part, turn) in enumerate(((1, 0), (2, 0), (1, 1), (2, 1), (0, 0), (0, 1))):
        span = pl.ds(channels(part, turn), BLOCK)
        parts[part, turn] = load(proj_hbm.at[span], proj.at[span], 1 + slot)
    later_loads = [
        load(source, target, 7 + slot)
        for slot, (source, target) in enumerate(
            (
                (grad_hbm, grad), (filt_hbm, filt), (spread_hbm, spread), (cos_hbm, cos_twist),
                (sin_hbm, sin_twist), (mix_hbm, mix), (gather_hbm, gather),
            )
        )
    ]

    gate = pltpu.get_barrier_semaphore()
    for step in range(1, 16):
        signal(gate, high * 16 + (low + step) % 16)
    for step in range(1, 16):
        signal(gate, ((high + step) % 16) * 16 + low)
    signal(gate, after)
    signal(gate, before)

    row = lax.broadcasted_iota(jnp.int32, (A, 128), 0)
    lane = lax.broadcasted_iota(jnp.int32, (A, 128), 1)
    for lag in range(1, TAPS):
        span = slice((lag - 1) * 128, lag * 128)
        shift[0, :, span] = (row == lane + 128 - lag).astype(F32).astype(BF16)
    last = one_hot((16, A), A - TAPS + 1, TAPS - 1)
    first = one_hot((16, A), 0, TAPS - 1)
    ahead = one_hot((16, 128), 128 - TAPS + 1, TAPS - 1)
    behind = one_hot((16, 128), 0, TAPS - 1)

    def take_edge(part, turn):
        parts[part, turn].wait()
        span = pl.ds(channels(part, turn), BLOCK)
        edge_out[0, :, span] = lax.dot_general(last, proj[span, :], NT, preferred_element_type=F32).astype(BF16)

    for part, turn in ((1, 0), (2, 0), (1, 1), (2, 1)):
        take_edge(part, turn)
    pl.semaphore_wait(gate, 32)
    tail = pl.ds(CH, 2 * CH)
    edge_kv = remote(edge_out.at[0, :, tail], edge_in.at[0, :, tail], sem_first, after)
    edge_kv.start()
    for step in range(1, 16):
        signal(rounds.at[0], ((high + step) % 16) * 16 + low)

    taps_load.wait()
    padded[...] = jnp.zeros_like(padded)
    padded[:TAPS, :] = taps[...].astype(F32)
    for block in range(0, 3 * CH, 128):
        weights[block : block + 128, :] = jnp.transpose(padded[:, block : block + 128])

    def filtered(part, turn, half):
        span = pl.ds(channels(part, turn), BLOCK)
        if half == 0:
            prior = lax.dot_general(edge_in[0, :, span], ahead, TN, preferred_element_type=F32).astype(BF16)
            prior = jnp.where(me > 0, prior, jnp.zeros_like(prior))
            window = jnp.concatenate([prior, proj[span, :128]], axis=1)
        else:
            window = proj[span, :]
        scale = weights[span, :]
        lanes = slice(half * 128, half * 128 + 128)
        moved = dot(window, shift[0])
        total = scale[:, 0:1] * proj[span, lanes].astype(F32)
        for lag in range(1, TAPS):
            total = total + scale[:, lag : lag + 1] * moved[:, (lag - 1) * 128 : lag * 128]
        total = total.astype(BF16)
        feat[span, lanes] = total
        return total.astype(F32)

    def chips(turn):
        return pl.ds(pl.multiple_of(channels(0, turn) // 8, SIDE), SIDE)

    def make_product(turn, half):
        keys = filtered(1, turn, half)
        values = filtered(2, turn, half)
        both = (keys * values).reshape(SIDE, 8, 128)
        prod[chips(turn), :, half * 128 : half * 128 + 128] = both.astype(BF16)

    def make_cotangent(turn, half):
        queries = filtered(0, turn, half)
        lanes = slice(half * 128, half * 128 + 128)
        both = (queries * grad[pl.ds(channels(0, turn), BLOCK), lanes].astype(F32)).reshape(SIDE, 8, 128)
        cotp[chips(turn), :, lanes] = both.astype(BF16)

    def send_side(source, target, sems, turn):
        base = (side * (1 - turn) + (1 - side) * turn) * SIDE

        def send(step, carry):
            other = base + (within + step) % SIDE
            remote(source.at[other], target.at[chip], sems.at[turn], other * 2 + core).start()
            return carry

        lax.fori_loop(1 - turn, SIDE, send, 0)

    def keep_own(source, target, slot):
        keep = pltpu.make_async_copy(source.at[chip], target.at[chip], own.at[slot])
        keep.start()
        return keep

    def settle_send(source, target, sems, turn):
        some = pl.ds(0, SIDE - 1 + turn)
        remote(source.at[some], target.at[some], sems.at[turn], ((chip + 1) % CHIPS) * 2 + core).wait_send()

    def settle_recv(source, target, sems, turn):
        some = pl.ds(0, SIDE - 1 + turn)
        remote(source.at[some], target.at[some], sems.at[turn], ((chip + 1) % CHIPS) * 2 + core).wait_recv()

    make_product(0, 1)
    edge_kv.wait()
    make_product(0, 0)
    pl.semaphore_wait(rounds.at[0], 15)
    send_side(prod, recv_p, sem_p, 0)
    keep_p = keep_own(prod, recv_p, 0)
    make_product(1, 1)
    make_product(1, 0)
    send_side(prod, recv_p, sem_p, 1)
    take_edge(0, 0)
    take_edge(0, 1)
    head = pl.ds(0, CH)
    edge_query = remote(edge_out.at[0, :, head], edge_in.at[0, :, head], sem_edge, after)
    edge_query.start()
    later_loads[0].wait()
    make_cotangent(0, 1)
    edge_query.wait()
    make_cotangent(0, 0)
    send_side(cotp, recv_g, sem_g, 0)
    keep_g = keep_own(cotp, recv_g, 1)
    make_cotangent(1, 1)
    make_cotangent(1, 0)
    send_side(cotp, recv_g, sem_g, 1)

    for copy in later_loads[1:]:
        copy.wait()
    mixback[:A, :A] = mix[:A, :A]
    mixback[A:, A:] = mix[A:, A:]
    mixback[:A, A:] = mix[A:, :A]
    mixback[A:, :A] = mix[:A, A:]
    for lag in range(1, TAPS):
        span = slice((lag - 1) * 128, lag * 128)
        shift[1, :, span] = (row == lane + lag).astype(F32).astype(BF16)

    def forward(signal_rows):
        raw = dot(spread[...], signal_rows)
        re, im, odd = raw[:HALF], raw[HALF : 2 * HALF], raw[2 * HALF :]
        ct, st = cos_twist[:HALF, :], sin_twist[:HALF, :]
        bins[:HALF, :A] = (re * ct + im * st).astype(BF16)
        bins[:HALF, A:] = (im * ct - re * st).astype(BF16)
        bins[HALF:, :A] = (odd * cos_twist[HALF:, :]).astype(BF16)
        bins[HALF:, A:] = (-odd * sin_twist[HALF:, :]).astype(BF16)
        return dot(bins[...], mix[...])

    def inverse(re, im):
        bins[:, :A] = re.astype(BF16)
        bins[:, A:] = im.astype(BF16)
        back = dot(bins[...], mixback[...])
        re, im = back[:, :A], back[:, A:]
        ct, st = cos_twist[...], sin_twist[...]
        turn_re = re * ct - im * st
        turn_im = im[:HALF] * ct[:HALF] + re[:HALF] * st[:HALF]
        top = lax.broadcasted_iota(jnp.int32, (16, A), 0) == 0
        rows[:HALF, :] = turn_re[:HALF].astype(BF16)
        rows[HALF:, :] = turn_im.astype(BF16)
        rows[HALF : HALF + 16, :] = jnp.where(top, turn_re[HALF:], turn_im[:16]).astype(BF16)
        return dot(gather[...], rows[...]) * (1.0 / PAD)

    def spread_filter(step, carry):
        piece = filt[:, pl.ds(pl.multiple_of(step * 1024, 1024), 1024)].astype(F32)
        fold[0, pl.ds(pl.multiple_of(step * 8, 8), 8), :] = piece.reshape(8, 128)
        return carry

    lax.fori_loop(0, SEQ // 1024, spread_filter, 0)
    for parity in range(2):
        for half in range(2):
            rows[parity * CHIPS : (parity + 1) * CHIPS, half * 128 : half * 128 + 128] = fold[
                0, pl.ds(2 * parity + half, CHIPS, stride=4), :
            ].astype(BF16)
    fspec[...] = forward(rows[:HALF, :])

    def swap_here(stream, channel, sems):
        return remote(
            swap_out.at[stream, channel], signals.at[stream * CPG + channel, mine, :], sems.at[channel], twin
        )

    def swap_back(stream, channel, sems):
        return remote(swap_out.at[2 + stream, channel], swap_in.at[stream, channel], sems.at[channel], twin)

    def unfold(received, stream, sems):
        for half in range(2):
            lanes = slice(half * 128, half * 128 + 128)
            fold[half] = received[:, :, lanes].astype(F32).reshape(CHIPS * 8, 128)
        for channel in range(CPG):
            for half in range(2):
                lanes = slice(half * 128, half * 128 + 128)
                low_set = fold[half, pl.ds(channel, CHIPS, stride=8), :]
                high_set = fold[half, pl.ds(CPG + channel, CHIPS, stride=8), :]
                signals[stream * CPG + channel, mine, lanes] = jnp.where(core == 0, low_set, high_set).astype(BF16)
                swap_out[stream, channel, :, lanes] = jnp.where(core == 0, high_set, low_set).astype(BF16)
            swap_here(stream, channel, sems).start()

    def refold(stream, ready, sems):
        for channel in range(CPG):
            swap_back(stream, channel, sems).wait()
            for half in range(2):
                lanes = slice(half * 128, half * 128 + 128)
                here = kept[stream, channel, :, lanes].astype(F32)
                there = swap_in[stream, channel, :, lanes].astype(F32)
                fold[half, pl.ds(channel, CHIPS, stride=8), :] = jnp.where(core == 0, here, there)
                fold[half, pl.ds(CPG + channel, CHIPS, stride=8), :] = jnp.where(core == 0, there, here)
        for half in range(2):
            ready[:, :, half * 128 : half * 128 + 128] = fold[half].reshape(CHIPS, 8, 128).astype(BF16)

    def put_away(result, stream, channel, sems):
        even, odd = result[:CHIPS], result[CHIPS:]
        kept[stream, channel] = jnp.where(core == 0, even, odd).astype(BF16)
        swap_out[2 + stream, channel] = jnp.where(core == 0, odd, even).astype(BF16)
        swap_back(stream, channel, sems).start()

    keep_p.wait()
    for turn in range(2):
        settle_recv(prod, recv_p, sem_p, turn)
    unfold(recv_p, 0, swap_p)

    def convolve(channel, carry):
        swap_here(0, channel, swap_p).wait()
        spec = forward(signals[channel])
        kspec[channel] = spec
        re, im = spec[:, :A], spec[:, A:]
        f_re, f_im = fspec[:, :A], fspec[:, A:]
        result = inverse((f_re * re - f_im * im) * SCALE, (f_re * im + f_im * re) * SCALE)
        put_away(result, 0, channel, swap_c)
        return carry

    lax.fori_loop(0, CPG, convolve, 0)
    refold(0, ready_c, swap_c)
    for turn in range(2):
        send_side(ready_c, tok_c, sem_c, turn)
    keep_c = keep_own(ready_c, tok_c, 2)

    keep_g.wait()
    for turn in range(2):
        settle_recv(cotp, recv_g, sem_g, turn)
    unfold(recv_g, 1, swap_g)
    cross[...] = jnp.zeros_like(cross)

    def correlate(channel, carry):
        swap_here(1, channel, swap_g).wait()
        spec = forward(signals[CPG + channel])
        re, im = spec[:, :A], spec[:, A:]
        k_re, k_im = kspec[channel, :, :A], kspec[channel, :, A:]
        cross[:, :A] = cross[:, :A] + (k_re * re + k_im * im)
        cross[:, A:] = cross[:, A:] + (k_re * im - k_im * re)
        f_re, f_im = fspec[:, :A], fspec[:, A:]
        result = inverse((f_re * re + f_im * im) * SCALE, (f_re * im - f_im * re) * SCALE)
        put_away(result, 1, channel, swap_b)
        return carry

    lax.fori_loop(0, CPG, correlate, 0)
    refold(1, ready_b, swap_b)
    for turn in range(2):
        send_side(ready_b, tok_b, sem_b, turn)
    keep_b = keep_own(ready_b, tok_b, 3)

    result = inverse(cross[:, :A], cross[:, A:]) * SCALE
    for parity in range(2):
        for half in range(2):
            fgrad[pl.ds(2 * parity + half, CHIPS, stride=4), :] = result[
                parity * CHIPS : (parity + 1) * CHIPS, half * 128 : half * 128 + 128
            ]

    keep_c.wait()
    for turn in range(2):
        settle_recv(ready_c, tok_c, sem_c, turn)

    def use_conv(step, carry):
        span = pl.ds(pl.multiple_of(step * BLOCK, BLOCK), BLOCK)
        conv = tok_c[pl.ds(step * SIDE, SIDE)].astype(F32).reshape(BLOCK, A)
        mixed[span, :] = (feat[span, :].astype(F32) * conv).astype(BF16)
        back = (grad[span, :].astype(F32) * conv).astype(BF16)
        dfeat[span, :] = back
        edge_q[0, :, span] = lax.dot_general(first, back, NT, preferred_element_type=F32).astype(BF16)
        return carry

    lax.fori_loop(0, CH // BLOCK, use_conv, 0)
    edge_back = remote(edge_q.at[0], edge_q.at[1], sem_edge_q, before)
    edge_back.start()

    def gathered(start, half, halo):
        span = pl.ds(pl.multiple_of(start, BLOCK), BLOCK)
        lanes = slice(half * 128, half * 128 + 128)
        if half == 0:
            window = dfeat[span, :]
        else:
            later = lax.dot_general(halo, behind, TN, preferred_element_type=F32).astype(BF16)
            later = jnp.where(me < DEVICES - 1, later, jnp.zeros_like(later))
            window = jnp.concatenate([dfeat[span, 128:], later], axis=1)
        scale = weights[span, :]
        moved = dot(window, shift[1])
        total = scale[:, 0:1] * dfeat[span, lanes].astype(F32)
        for lag in range(1, TAPS):
            total = total + scale[:, lag : lag + 1] * moved[:, (lag - 1) * 128 : lag * 128]
        pgrad[span, lanes] = total.astype(BF16)

    for step in range(CH // BLOCK):
        gathered(step * BLOCK, 0, None)
    edge_back.wait()
    for step in range(CH // BLOCK):
        gathered(step * BLOCK, 1, edge_q[1, :, step * BLOCK : (step + 1) * BLOCK])

    def use_back(turn, sems):
        back = tok_b[chips(turn)].astype(F32).reshape(BLOCK, A)
        for part, other in ((1, 2), (2, 1)):
            result = (feat[pl.ds(channels(other, turn), BLOCK), :].astype(F32) * back).astype(BF16)
            target = pl.ds(channels(part, turn), BLOCK)
            dfeat[target, :] = result
            edge_out[1, :, target] = lax.dot_general(first, result, NT, preferred_element_type=F32).astype(BF16)
        edges = []
        for part in (1, 2):
            target = pl.ds(channels(part, turn), BLOCK)
            edge = remote(edge_out.at[1, :, target], edge_in.at[1, :, target], sems.at[part - 1], before)
            edge.start()
            edges.append(edge)
        return edges

    keep_b.wait()
    settle_recv(ready_b, tok_b, sem_b, 0)
    edges = use_back(0, sem_edge_own)
    for part in (1, 2):
        gathered(channels(part, 0), 0, None)
    settle_recv(ready_b, tok_b, sem_b, 1)
    edges += use_back(1, sem_edge_rest)
    for part in (1, 2):
        gathered(channels(part, 1), 0, None)
    for source, target, sems in ((prod, recv_p, sem_p), (cotp, recv_g, sem_g), (ready_c, tok_c, sem_c), (ready_b, tok_b, sem_b)):
        for turn in range(2):
            settle_send(source, target, sems, turn)
    for edge in edges:
        edge.wait()
    for turn in range(2):
        for part in (1, 2):
            gathered(channels(part, turn), 1, edge_in[1, :, pl.ds(channels(part, turn), BLOCK)])


def shards(projections, short_filter, long_filter, out_grad):
    vmem = pl.BlockSpec(memory_space=pltpu.VMEM)
    hbm = pl.BlockSpec(memory_space=pltpu.HBM)
    tokens = pltpu.VMEM((CHIPS, 8, A), BF16)
    pair = pltpu.SemaphoreType.DMA((2,))
    sides = pltpu.SemaphoreType.DMA((2, 2))
    swaps = pltpu.SemaphoreType.DMA((CPG, 2))
    operands = (projections, short_filter, long_filter, out_grad, *make_tables())
    mixed, proj_grad, filter_grad = pl.pallas_call(
        mixer_kernel,
        out_shape=(
            jax.ShapeDtypeStruct((CH, A), BF16),
            jax.ShapeDtypeStruct((3 * CH, A), BF16),
            jax.ShapeDtypeStruct((SEQ // 128, 128), F32),
        ),
        in_specs=[hbm] * 9,
        out_specs=(vmem, vmem, vmem),
        scratch_shapes=[
            *[pltpu.VMEM(operand.shape, operand.dtype) for operand in operands],
            pltpu.VMEM((8, 3 * CH), F32),
            pltpu.VMEM((3 * CH, 8), F32),
            pltpu.VMEM((2, A, 128 * (TAPS - 1)), BF16),
            pltpu.VMEM((3 * CH, A), BF16),
            tokens, tokens, tokens, tokens,
            pltpu.VMEM((2, CHIPS * 8, 128), F32),
            pltpu.VMEM((2 * CPG, HALF, A), BF16),
            pltpu.VMEM((4, CPG, CHIPS, A), BF16),
            pltpu.VMEM((2, CPG, CHIPS, A), BF16),
            pltpu.VMEM((2, CPG, CHIPS, A), BF16),
            tokens, tokens, tokens, tokens,
            pltpu.VMEM((ROWS, 2 * A), F32),
            pltpu.VMEM((CPG, ROWS, 2 * A), F32),
            pltpu.VMEM((ROWS, 2 * A), F32),
            pltpu.VMEM((ROWS, 2 * A), BF16),
            pltpu.VMEM((2 * HALF, A), BF16),
            pltpu.VMEM((2 * A, 2 * A), BF16),
            pltpu.VMEM((3 * CH, A), BF16),
            pltpu.VMEM((2, 16, 3 * CH), BF16),
            pltpu.VMEM((2, 16, 3 * CH), BF16),
            pltpu.VMEM((2, 16, CH), BF16),
            pltpu.SemaphoreType.REGULAR((1,)),
            pltpu.SemaphoreType.DMA((14,)),
            pair, pair, sides, sides, pair, sides, sides, sides, sides,
            swaps, swaps, swaps, swaps,
            pltpu.SemaphoreType.DMA((4,)),
        ],
        compiler_params=pltpu.CompilerParams(collective_id=0, has_side_effects=True, vmem_limit_bytes=44 << 20),
        name="mixer",
    )(*[pltpu.with_memory_space_constraint(operand, pltpu.HBM) for operand in operands])
    return (mixed, proj_grad, filter_grad.reshape(1, SEQ))


def solution(mesh):
    placed = (P(None, ("dp", "ctx")), P(), P(("dp", "ctx"), None), P(None, ("dp", "ctx")))
    return jax.shard_map(
        shards,
        mesh=mesh,
        in_specs=placed,
        out_specs=(P(None, ("dp", "ctx")), P(None, ("dp", "ctx")), P(("dp", "ctx"), None)),
        check_vma=False,
    )
```

time: 87.2 us -> 77.3 us (0.89)
  Pallas kernels: 77.5 us -> 73.9 us
  other arithmetic: 3.12 us -> 0 us
  local copies, waits for them, and re-layouts: 5.76 us -> 2.64 us
    pallas_call x1, Pallas kernels: 77.5 us -> 73.9 us  [shards(): pl.pallas_call(mixer_kernel, out_shape=(jax.ShapeDtypeStruct((CH, A), BF1...]
    unnamed x5 -> x3, local copies, waits for them, and re-layouts: 5.05 us -> 2.64 us
    unnamed x1 -> x0, other arithmetic: 1.67 us -> none
    pad x1 -> x0, other arithmetic: 1.45 us -> none  [shards(): taps = jnp.pad(short_filter.astype(F32), ((0, 8 - TAPS), (0, 0)))]
where the time goes in v1:
time: 77.3 us; the launch traced here: 77.2 us
  Pallas kernels  73.9 us (96%)
  local copies, waits for them, and re-layouts  2.64 us (3%)
    pallas_call x1, Pallas kernels, shards(): pl.pallas_call(mixer_kernel, out_shape=(jax.ShapeDtypeStruct((CH, A), BF1...  73.9 us
    unnamed x3, local copies, waits for them, and re-layouts  2.64 us

profile of v1, /device:TPU:1, one launch (start us, length us, event | category | flops | bytes accessed | tf_op | source)
XLA Modules:
  0.0 77.2 jit_solution(13562095414653575234)
XLA Ops:
  0.6 73.9 %mixer.1 = (bf16[1024,256]{1,0:T(8,128)(2,1)S(1)}, bf16[3072,256]{1,0:T(8,128)(2,1)S(1)}, f32[512,128]{1,0:T(8,128)S(1)}) custom-call(bf16[3072,256]{1,0:T(8,128)(2,1)} %proj_hbm.1, bf16[7,3072]{1,0:T(8,128)(2,1)} %taps_hbm.1, bf16[1,65536]{1,0:T(2,128)(2,1)} %filt_hbm.1, bf16[1024,256]{1,0:T(8,128)(2,1)} %grad_hbm.1, ...), custom_call_target="tpu_custom_call" | custom-call | tf_op jit(solution)/shard_map/mixer/pallas_call | solution.py:463
  74.5 0.8 %copy.15 = bf16[1024,256]{1,0:T(8,128)(2,1)} copy(bf16[1024,256]{1,0:T(8,128)(2,1)S(1)} %get-tuple-element.12) | data formatting | bytes 1048576
  75.3 1.1 %copy.16 = bf16[3072,256]{1,0:T(8,128)(2,1)} copy(bf16[3072,256]{1,0:T(8,128)(2,1)S(1)} %get-tuple-element.13) | data formatting | bytes 3145728
  76.5 0.7 copy.17

commit v2 on v1

--- a/solution.py
+++ b/solution.py
@@ -113,6 +113,14 @@
     for slot, (part, turn) in enumerate(((1, 0), (2, 0), (1, 1), (2, 1), (0, 0), (0, 1))):
         span = pl.ds(channels(part, turn), BLOCK)
         parts[part, turn] = load(proj_hbm.at[span], proj.at[span], 1 + slot)
+    gate = pltpu.get_barrier_semaphore()
+    for step in range(1, 16):
+        signal(gate, high * 16 + (low + step) % 16)
+    for step in range(1, 16):
+        signal(gate, ((high + step) % 16) * 16 + low)
+    signal(gate, after)
+    signal(gate, before)
+
     later_loads = [
         load(source, target, 7 + slot)
         for slot, (source, target) in enumerate(
@@ -123,14 +131,6 @@
         )
     ]
 
-    gate = pltpu.get_barrier_semaphore()
-    for step in range(1, 16):
-        signal(gate, high * 16 + (low + step) % 16)
-    for step in range(1, 16):
-        signal(gate, ((high + step) % 16) * 16 + low)
-    signal(gate, after)
-    signal(gate, before)
-
     row = lax.broadcasted_iota(jnp.int32, (A, 128), 0)
     lane = lax.broadcasted_iota(jnp.int32, (A, 128), 1)
     for lag in range(1, TAPS):
@@ -141,6 +141,12 @@
     ahead = one_hot((16, 128), 128 - TAPS + 1, TAPS - 1)
     behind = one_hot((16, 128), 0, TAPS - 1)
 
+    taps_load.wait()
+    padded[...] = jnp.zeros_like(padded)
+    padded[:TAPS, :] = taps[...].astype(F32)
+    for block in range(0, 3 * CH, 128):
+        weights[block : block + 128, :] = jnp.transpose(padded[:, block : block + 128])
+
     def take_edge(part, turn):
         parts[part, turn].wait()
         span = pl.ds(channels(part, turn), BLOCK)
@@ -154,12 +160,6 @@
     edge_kv.start()
     for step in range(1, 16):
         signal(rounds.at[0], ((high + step) % 16) * 16 + low)
-
-    taps_load.wait()
-    padded[...] = jnp.zeros_like(padded)
-    padded[:TAPS, :] = taps[...].astype(F32)
-    for block in range(0, 3 * CH, 128):
-        weights[block : block + 128, :] = jnp.transpose(padded[:, block : block + 128])
 
     def filtered(part, turn, half):
         span = pl.ds(channels(part, turn), BLOCK)
@@ -450,6 +450,31 @@
     for turn in range(2):
         for part in (1, 2):
             gathered(channels(part, turn), 1, edge_in[1, :, pl.ds(channels(part, turn), BLOCK)])
+
+
+def write_kernel(mixed_in, pgrad_in, fgrad_in, mixed, pgrad, fgrad, sems):
+    copies = [pltpu.make_async_copy(fgrad_in, fgrad, sems.at[0]), pltpu.make_async_copy(mixed_in, mixed, sems.at[1])]
+    for part in range(3):
+        span = pl.ds(part * CH, CH)
+        copies.append(pltpu.make_async_copy(pgrad_in.at[span], pgrad.at[span], sems.at[2 + part]))
+    for copy in copies:
+        copy.start()
+    for copy in copies:
+        copy.wait()
+
+
+def write_out(*results):
+    anywhere = pl.BlockSpec(memory_space=pl.ANY)
+    hbm = pl.BlockSpec(memory_space=pltpu.HBM)
+    return pl.pallas_call(
+        write_kernel,
+        out_shape=tuple(pltpu.HBM(result.shape, result.dtype) for result in results),
+        in_specs=[anywhere] * 3,
+        out_specs=(hbm,) * 3,
+        scratch_shapes=[pltpu.SemaphoreType.DMA((5,))],
+        compiler_params=pltpu.CompilerParams(vmem_limit_bytes=1 << 20),
+        name="write_out",
+    )(*results)
 
 
 def shards(projections, short_filter, long_filter, out_grad):
@@ -501,6 +526,7 @@
         compiler_params=pltpu.CompilerParams(collective_id=0, has_side_effects=True, vmem_limit_bytes=44 << 20),
         name="mixer",
     )(*[pltpu.with_memory_space_constraint(operand, pltpu.HBM) for operand in operands])
+    mixed, proj_grad, filter_grad = write_out(mixed, proj_grad, filter_grad)
     return (mixed, proj_grad, filter_grad.reshape(1, SEQ))
 
 

time: 77.3 us -> 76.2 us (0.986)
  local copies, waits for them, and re-layouts: 2.64 us -> 0 us
  Pallas kernels: 73.9 us -> 75.3 us
    unnamed x3 -> x0, local copies, waits for them, and re-layouts: 2.64 us -> none
    pallas_call x0 -> x1, Pallas kernels: none -> 1.44 us  [write_out(): pl.pallas_call(write_kernel, out_shape=tuple((pltpu.HBM(result.shape, res...]
where the time goes in v2:
time: 76.2 us; the launch traced here: 76.1 us
  Pallas kernels  75.3 us (99%)
  between operations  0.8 us (1%)
    pallas_call x1, Pallas kernels, shards(): pl.pallas_call(mixer_kernel, out_shape=(jax.ShapeDtypeStruct((CH, A), BF1...  73.9 us

profile of v2, /device:TPU:1, one launch (start us, length us, event | category | flops | bytes accessed | tf_op | source)
XLA Modules:
  0.0 76.1 jit_solution(4959103937845502479)
XLA Ops:
  0.6 73.9 %mixer.1 = (bf16[1024,256]{1,0:T(8,128)(2,1)S(1)}, bf16[3072,256]{1,0:T(8,128)(2,1)S(1)}, f32[512,128]{1,0:T(8,128)S(1)}) custom-call(bf16[3072,256]{1,0:T(8,128)(2,1)} %proj_hbm.1, bf16[7,3072]{1,0:T(8,128)(2,1)} %taps_hbm.1, bf16[1,65536]{1,0:T(2,128)(2,1)} %filt_hbm.1, bf16[1024,256]{1,0:T(8,128)(2,1)} %grad_hbm.1, ...), custom_call_target="tpu_custom_call" | custom-call | tf_op jit(solution)/shard_map/mixer/pallas_call | solution.py:488
  74.5 1.4 %write_out.1 = (bf16[1024,256]{1,0:T(8,128)(2,1)}, bf16[3072,256]{1,0:T(8,128)(2,1)}, f32[512,128]{1,0:T(8,128)}) custom-call(bf16[1024,256]{1,0:T(8,128)(2,1)S(1)} %get-tuple-element.9.mixed_in, bf16[3072,256]{1,0:T(8,128)(2,1)S(1)} %get-tuple-element.10.pgrad_in, f32[512,128]{1,0:T(8,128)S(1)} %get-tuple-element.11.fgrad_in), custom_call_target="tpu_custom_call" | custom-call | tf_op jit(solution)/shard_map/write_out/pallas_call | solution.py:469

commit v3 on v2

--- a/solution.py
+++ b/solution.py
@@ -127,6 +127,8 @@
             (
                 (grad_hbm, grad), (filt_hbm, filt), (spread_hbm, spread), (cos_hbm, cos_twist),
                 (sin_hbm, sin_twist), (mix_hbm, mix), (gather_hbm, gather),
+                (mix_hbm.at[:A, :A], mixback.at[:A, :A]), (mix_hbm.at[A:, A:], mixback.at[A:, A:]),
+                (mix_hbm.at[A:, :A], mixback.at[:A, A:]), (mix_hbm.at[:A, A:], mixback.at[A:, :A]),
             )
         )
     ]
@@ -197,12 +199,15 @@
     def send_side(source, target, sems, turn):
         base = (side * (1 - turn) + (1 - side) * turn) * SIDE
 
+        batch = 7 + turn
+
         def send(step, carry):
-            other = base + (within + step) % SIDE
-            remote(source.at[other], target.at[chip], sems.at[turn], other * 2 + core).start()
+            for place_in_batch in range(batch):
+                other = base + (within + step * batch + place_in_batch + 1 - turn) % SIDE
+                remote(source.at[other], target.at[chip], sems.at[turn], other * 2 + core).start()
             return carry
 
-        lax.fori_loop(1 - turn, SIDE, send, 0)
+        lax.fori_loop(0, (SIDE - 1 + turn) // batch, send, 0)
 
     def keep_own(source, target, slot):
         keep = pltpu.make_async_copy(source.at[chip], target.at[chip], own.at[slot])
@@ -243,13 +248,6 @@
 
     for copy in later_loads[1:]:
         copy.wait()
-    mixback[:A, :A] = mix[:A, :A]
-    mixback[A:, A:] = mix[A:, A:]
-    mixback[:A, A:] = mix[A:, :A]
-    mixback[A:, :A] = mix[:A, A:]
-    for lag in range(1, TAPS):
-        span = slice((lag - 1) * 128, lag * 128)
-        shift[1, :, span] = (row == lane + lag).astype(F32).astype(BF16)
 
     def forward(signal_rows):
         raw = dot(spread[...], signal_rows)
@@ -353,6 +351,9 @@
         settle_recv(cotp, recv_g, sem_g, turn)
     unfold(recv_g, 1, swap_g)
     cross[...] = jnp.zeros_like(cross)
+    for lag in range(1, TAPS):
+        span = slice((lag - 1) * 128, lag * 128)
+        shift[1, :, span] = (row == lane + lag).astype(F32).astype(BF16)
 
     def correlate(channel, carry):
         swap_here(1, channel, swap_g).wait()
@@ -438,18 +439,33 @@
     edges = use_back(0, sem_edge_own)
     for part in (1, 2):
         gathered(channels(part, 0), 0, None)
+
+    ahead_side = after // 2 // SIDE
+    first_start = ahead_side * BLOCK
+    second_start = (1 - ahead_side) * BLOCK
+
+    def finish(start):
+        for part in (1, 2):
+            begin = pl.multiple_of(part * CH + start, BLOCK)
+            gathered(begin, 1, edge_in[1, :, pl.ds(begin, BLOCK)])
+
+    for edge in edges:
+        edge.wait()
+    finish(first_start)
     settle_recv(ready_b, tok_b, sem_b, 1)
-    edges += use_back(1, sem_edge_rest)
+    edges_rest = use_back(1, sem_edge_rest)
     for part in (1, 2):
         gathered(channels(part, 1), 0, None)
     for source, target, sems in ((prod, recv_p, sem_p), (cotp, recv_g, sem_g), (ready_c, tok_c, sem_c), (ready_b, tok_b, sem_b)):
         for turn in range(2):
             settle_send(source, target, sems, turn)
-    for edge in edges:
+    for edge in edges_rest:
         edge.wait()
-    for turn in range(2):
-        for part in (1, 2):
-            gathered(channels(part, turn), 1, edge_in[1, :, pl.ds(channels(part, turn), BLOCK)])
+    finish(second_start)
+
+    @pl.when(ahead_side != side)
+    def _():
+        finish(first_start)
 
 
 def write_kernel(mixed_in, pgrad_in, fgrad_in, mixed, pgrad, fgrad, sems):
@@ -518,7 +534,7 @@
             pltpu.VMEM((2, 16, 3 * CH), BF16),
             pltpu.VMEM((2, 16, CH), BF16),
             pltpu.SemaphoreType.REGULAR((1,)),
-            pltpu.SemaphoreType.DMA((14,)),
+            pltpu.SemaphoreType.DMA((18,)),
             pair, pair, sides, sides, pair, sides, sides, sides, sides,
             swaps, swaps, swaps, swaps,
             pltpu.SemaphoreType.DMA((4,)),

time: 76.2 us -> 73.5 us (0.965)
  Pallas kernels: 75.3 us -> 72.6 us
    pallas_call x1, Pallas kernels: 73.9 us -> 71.2 us  [shards(): pl.pallas_call(mixer_kernel, out_shape=(jax.ShapeDtypeStruct((CH, A), BF1...]
where the time goes in v3:
time: 73.5 us; the launch traced here: 73.4 us
  Pallas kernels  72.6 us (99%)
  between operations  0.82 us (1%)
    pallas_call x1, Pallas kernels, shards(): pl.pallas_call(mixer_kernel, out_shape=(jax.ShapeDtypeStruct((CH, A), BF1...  71.2 us

profile of v3, /device:TPU:1, one launch (start us, length us, event | category | flops | bytes accessed | tf_op | source)
XLA Modules:
  0.0 73.4 jit_solution(7887390631504733226)
XLA Ops:
  0.6 71.2 %mixer.1 = (bf16[1024,256]{1,0:T(8,128)(2,1)S(1)}, bf16[3072,256]{1,0:T(8,128)(2,1)S(1)}, f32[512,128]{1,0:T(8,128)S(1)}) custom-call(bf16[3072,256]{1,0:T(8,128)(2,1)} %proj_hbm.1, bf16[7,3072]{1,0:T(8,128)(2,1)} %taps_hbm.1, bf16[1,65536]{1,0:T(2,128)(2,1)} %filt_hbm.1, bf16[1024,256]{1,0:T(8,128)(2,1)} %grad_hbm.1, ...), custom_call_target="tpu_custom_call" | custom-call | tf_op jit(solution)/shard_map/mixer/pallas_call | solution.py:504
  71.8 1.4 %write_out.1 = (bf16[1024,256]{1,0:T(8,128)(2,1)}, bf16[3072,256]{1,0:T(8,128)(2,1)}, f32[512,128]{1,0:T(8,128)}) custom-call(bf16[1024,256]{1,0:T(8,128)(2,1)S(1)} %get-tuple-element.9.mixed_in, bf16[3072,256]{1,0:T(8,128)(2,1)S(1)} %get-tuple-element.10.pgrad_in, f32[512,128]{1,0:T(8,128)S(1)} %get-tuple-element.11.fgrad_in), custom_call_target="tpu_custom_call" | custom-call | tf_op jit(solution)/shard_map/write_out/pallas_call | solution.py:485

commit v4 on v3

--- a/solution.py
+++ b/solution.py
@@ -163,8 +163,10 @@
     for step in range(1, 16):
         signal(rounds.at[0], ((high + step) % 16) * 16 + low)
 
-    def filtered(part, turn, half):
+    def filtered(part, turn, half, quarter=None):
         span = pl.ds(channels(part, turn), BLOCK)
+        if quarter is not None:
+            span = pl.ds(pl.multiple_of(channels(part, turn) + quarter * (BLOCK // 2), BLOCK // 2), BLOCK // 2)
         if half == 0:
             prior = lax.dot_general(edge_in[0, :, span], ahead, TN, preferred_element_type=F32).astype(BF16)
             prior = jnp.where(me > 0, prior, jnp.zeros_like(prior))
@@ -184,11 +186,14 @@
     def chips(turn):
         return pl.ds(pl.multiple_of(channels(0, turn) // 8, SIDE), SIDE)
 
-    def make_product(turn, half):
-        keys = filtered(1, turn, half)
-        values = filtered(2, turn, half)
-        both = (keys * values).reshape(SIDE, 8, 128)
-        prod[chips(turn), :, half * 128 : half * 128 + 128] = both.astype(BF16)
+    def make_product(turn, half, quarter=None):
+        keys = filtered(1, turn, half, quarter)
+        values = filtered(2, turn, half, quarter)
+        where = chips(turn)
+        if quarter is not None:
+            where = pl.ds(pl.multiple_of(channels(0, turn) // 8 + quarter * (SIDE // 2), SIDE // 2), SIDE // 2)
+        both = (keys * values).reshape(-1, 8, 128)
+        prod[where, :, half * 128 : half * 128 + 128] = both.astype(BF16)
 
     def make_cotangent(turn, half):
         queries = filtered(0, turn, half)
@@ -209,6 +214,16 @@
 
         lax.fori_loop(0, (SIDE - 1 + turn) // batch, send, 0)
 
+    def send_quarter(source, target, sems, quarter, skip):
+        base = side * SIDE + quarter * (SIDE // 2)
+
+        def send(step, carry):
+            other = base + (within + step) % (SIDE // 2)
+            remote(source.at[other], target.at[chip], sems.at[0], other * 2 + core).start()
+            return carry
+
+        lax.fori_loop(skip, SIDE // 2, send, 0)
+
     def keep_own(source, target, slot):
         keep = pltpu.make_async_copy(source.at[chip], target.at[chip], own.at[slot])
         keep.start()
@@ -222,12 +237,16 @@
         some = pl.ds(0, SIDE - 1 + turn)
         remote(source.at[some], target.at[some], sems.at[turn], ((chip + 1) % CHIPS) * 2 + core).wait_recv()
 
-    make_product(0, 1)
+    near = within // (SIDE // 2)
+    make_product(0, 1, near)
     edge_kv.wait()
-    make_product(0, 0)
+    make_product(0, 0, near)
     pl.semaphore_wait(rounds.at[0], 15)
-    send_side(prod, recv_p, sem_p, 0)
+    send_quarter(prod, recv_p, sem_p, near, 1)
     keep_p = keep_own(prod, recv_p, 0)
+    make_product(0, 1, 1 - near)
+    make_product(0, 0, 1 - near)
+    send_quarter(prod, recv_p, sem_p, 1 - near, 0)
     make_product(1, 1)
     make_product(1, 0)
     send_side(prod, recv_p, sem_p, 1)
@@ -249,29 +268,32 @@
     for copy in later_loads[1:]:
         copy.wait()
 
-    def forward(signal_rows):
-        raw = dot(spread[...], signal_rows)
-        re, im, odd = raw[:HALF], raw[HALF : 2 * HALF], raw[2 * HALF :]
+    def forward(signals_rows):
+        raws = [dot(spread[...], signal_rows) for signal_rows in signals_rows]
         ct, st = cos_twist[:HALF, :], sin_twist[:HALF, :]
-        bins[:HALF, :A] = (re * ct + im * st).astype(BF16)
-        bins[:HALF, A:] = (im * ct - re * st).astype(BF16)
-        bins[HALF:, :A] = (odd * cos_twist[HALF:, :]).astype(BF16)
-        bins[HALF:, A:] = (-odd * sin_twist[HALF:, :]).astype(BF16)
-        return dot(bins[...], mix[...])
-
-    def inverse(re, im):
-        bins[:, :A] = re.astype(BF16)
-        bins[:, A:] = im.astype(BF16)
-        back = dot(bins[...], mixback[...])
-        re, im = back[:, :A], back[:, A:]
+        for slot, raw in enumerate(raws):
+            re, im, odd = raw[:HALF], raw[HALF : 2 * HALF], raw[2 * HALF :]
+            bins[slot, :HALF, :A] = (re * ct + im * st).astype(BF16)
+            bins[slot, :HALF, A:] = (im * ct - re * st).astype(BF16)
+            bins[slot, HALF:, :A] = (odd * cos_twist[HALF:, :]).astype(BF16)
+            bins[slot, HALF:, A:] = (-odd * sin_twist[HALF:, :]).astype(BF16)
+        return [dot(bins[slot], mix[...]) for slot in range(len(raws))]
+
+    def inverse(spectra):
+        for slot, (re, im) in enumerate(spectra):
+            bins[slot, :, :A] = re.astype(BF16)
+            bins[slot, :, A:] = im.astype(BF16)
+        backs = [dot(bins[slot], mixback[...]) for slot in range(len(spectra))]
         ct, st = cos_twist[...], sin_twist[...]
-        turn_re = re * ct - im * st
-        turn_im = im[:HALF] * ct[:HALF] + re[:HALF] * st[:HALF]
         top = lax.broadcasted_iota(jnp.int32, (16, A), 0) == 0
-        rows[:HALF, :] = turn_re[:HALF].astype(BF16)
-        rows[HALF:, :] = turn_im.astype(BF16)
-        rows[HALF : HALF + 16, :] = jnp.where(top, turn_re[HALF:], turn_im[:16]).astype(BF16)
-        return dot(gather[...], rows[...]) * (1.0 / PAD)
+        for slot, back in enumerate(backs):
+            re, im = back[:, :A], back[:, A:]
+            turn_re = re * ct - im * st
+            turn_im = im[:HALF] * ct[:HALF] + re[:HALF] * st[:HALF]
+            rows[slot, :HALF, :] = turn_re[:HALF].astype(BF16)
+            rows[slot, HALF:, :] = turn_im.astype(BF16)
+            rows[slot, HALF : HALF + 16, :] = jnp.where(top, turn_re[HALF:], turn_im[:16]).astype(BF16)
+        return [dot(gather[...], rows[slot]) * (1.0 / PAD) for slot in range(len(spectra))]
 
     def spread_filter(step, carry):
         piece = filt[:, pl.ds(pl.multiple_of(step * 1024, 1024), 1024)].astype(F32)
@@ -281,10 +303,10 @@
     lax.fori_loop(0, SEQ // 1024, spread_filter, 0)
     for parity in range(2):
         for half in range(2):
-            rows[parity * CHIPS : (parity + 1) * CHIPS, half * 128 : half * 128 + 128] = fold[
+            rows[0, parity * CHIPS : (parity + 1) * CHIPS, half * 128 : half * 128 + 128] = fold[
                 0, pl.ds(2 * parity + half, CHIPS, stride=4), :
             ].astype(BF16)
-    fspec[...] = forward(rows[:HALF, :])
+    fspec[...] = forward([rows[0, :HALF, :]])[0]
 
     def swap_here(stream, channel, sems):
         return remote(
@@ -330,17 +352,21 @@
         settle_recv(prod, recv_p, sem_p, turn)
     unfold(recv_p, 0, swap_p)
 
-    def convolve(channel, carry):
-        swap_here(0, channel, swap_p).wait()
-        spec = forward(signals[channel])
-        kspec[channel] = spec
-        re, im = spec[:, :A], spec[:, A:]
-        f_re, f_im = fspec[:, :A], fspec[:, A:]
-        result = inverse((f_re * re - f_im * im) * SCALE, (f_re * im + f_im * re) * SCALE)
-        put_away(result, 0, channel, swap_c)
+    def convolve(step, carry):
+        pair = [step * 2, step * 2 + 1]
+        for channel in pair:
+            swap_here(0, channel, swap_p).wait()
+        spectra = []
+        for channel, spec in zip(pair, forward([signals[channel] for channel in pair])):
+            kspec[channel] = spec
+            re, im = spec[:, :A], spec[:, A:]
+            f_re, f_im = fspec[:, :A], fspec[:, A:]
+            spectra.append(((f_re * re - f_im * im) * SCALE, (f_re * im + f_im * re) * SCALE))
+        for channel, result in zip(pair, inverse(spectra)):
+            put_away(result, 0, channel, swap_c)
         return carry
 
-    lax.fori_loop(0, CPG, convolve, 0)
+    lax.fori_loop(0, CPG // 2, convolve, 0)
     refold(0, ready_c, swap_c)
     for turn in range(2):
         send_side(ready_c, tok_c, sem_c, turn)
@@ -355,25 +381,29 @@
         span = slice((lag - 1) * 128, lag * 128)
         shift[1, :, span] = (row == lane + lag).astype(F32).astype(BF16)
 
-    def correlate(channel, carry):
-        swap_here(1, channel, swap_g).wait()
-        spec = forward(signals[CPG + channel])
-        re, im = spec[:, :A], spec[:, A:]
-        k_re, k_im = kspec[channel, :, :A], kspec[channel, :, A:]
-        cross[:, :A] = cross[:, :A] + (k_re * re + k_im * im)
-        cross[:, A:] = cross[:, A:] + (k_re * im - k_im * re)
-        f_re, f_im = fspec[:, :A], fspec[:, A:]
-        result = inverse((f_re * re + f_im * im) * SCALE, (f_re * im - f_im * re) * SCALE)
-        put_away(result, 1, channel, swap_b)
+    def correlate(step, carry):
+        pair = [step * 2, step * 2 + 1]
+        for channel in pair:
+            swap_here(1, channel, swap_g).wait()
+        spectra = []
+        for channel, spec in zip(pair, forward([signals[CPG + channel] for channel in pair])):
+            re, im = spec[:, :A], spec[:, A:]
+            k_re, k_im = kspec[channel, :, :A], kspec[channel, :, A:]
+            cross[:, :A] = cross[:, :A] + (k_re * re + k_im * im)
+            cross[:, A:] = cross[:, A:] + (k_re * im - k_im * re)
+            f_re, f_im = fspec[:, :A], fspec[:, A:]
+            spectra.append(((f_re * re + f_im * im) * SCALE, (f_re * im - f_im * re) * SCALE))
+        for channel, result in zip(pair, inverse(spectra)):
+            put_away(result, 1, channel, swap_b)
         return carry
 
-    lax.fori_loop(0, CPG, correlate, 0)
+    lax.fori_loop(0, CPG // 2, correlate, 0)
     refold(1, ready_b, swap_b)
     for turn in range(2):
         send_side(ready_b, tok_b, sem_b, turn)
     keep_b = keep_own(ready_b, tok_b, 3)
 
-    result = inverse(cross[:, :A], cross[:, A:]) * SCALE
+    result = inverse([(cross[:, :A], cross[:, A:])])[0] * SCALE
     for parity in range(2):
         for half in range(2):
             fgrad[pl.ds(2 * parity + half, CHIPS, stride=4), :] = result[
@@ -526,8 +556,8 @@
             pltpu.VMEM((ROWS, 2 * A), F32),
             pltpu.VMEM((CPG, ROWS, 2 * A), F32),
             pltpu.VMEM((ROWS, 2 * A), F32),
-            pltpu.VMEM((ROWS, 2 * A), BF16),
-            pltpu.VMEM((2 * HALF, A), BF16),
+            pltpu.VMEM((2, ROWS, 2 * A), BF16),
+            pltpu.VMEM((2, 2 * HALF, A), BF16),
             pltpu.VMEM((2 * A, 2 * A), BF16),
             pltpu.VMEM((3 * CH, A), BF16),
             pltpu.VMEM((2, 16, 3 * CH), BF16),

time: 73.5 us -> 72.5 us (0.986)
  Pallas kernels: 72.6 us -> 71.6 us
    pallas_call x1, Pallas kernels: 71.2 us -> 70.1 us  [shards(): pl.pallas_call(mixer_kernel, out_shape=(jax.ShapeDtypeStruct((CH, A), BF1...]
where the time goes in v4:
time: 72.5 us; the launch traced here: 72.4 us
  Pallas kernels  71.6 us (99%)
  between operations  0.82 us (1%)
    pallas_call x1, Pallas kernels, shards(): pl.pallas_call(mixer_kernel, out_shape=(jax.ShapeDtypeStruct((CH, A), BF1...  70.1 us

profile of v4, /device:TPU:1, one launch (start us, length us, event | category | flops | bytes accessed | tf_op | source)
XLA Modules:
  0.0 72.4 jit_solution(18396026683214626814)
XLA Ops:
  0.6 70.1 %mixer.1 = (bf16[1024,256]{1,0:T(8,128)(2,1)S(1)}, bf16[3072,256]{1,0:T(8,128)(2,1)S(1)}, f32[512,128]{1,0:T(8,128)S(1)}) custom-call(bf16[3072,256]{1,0:T(8,128)(2,1)} %proj_hbm.1, bf16[7,3072]{1,0:T(8,128)(2,1)} %taps_hbm.1, bf16[1,65536]{1,0:T(2,128)(2,1)} %filt_hbm.1, bf16[1024,256]{1,0:T(8,128)(2,1)} %grad_hbm.1, ...), custom_call_target="tpu_custom_call" | custom-call | tf_op jit(solution)/shard_map/mixer/pallas_call | solution.py:534
  70.8 1.4 %write_out.1 = (bf16[1024,256]{1,0:T(8,128)(2,1)}, bf16[3072,256]{1,0:T(8,128)(2,1)}, f32[512,128]{1,0:T(8,128)}) custom-call(bf16[1024,256]{1,0:T(8,128)(2,1)S(1)} %get-tuple-element.9.mixed_in, bf16[3072,256]{1,0:T(8,128)(2,1)S(1)} %get-tuple-element.10.pgrad_in, f32[512,128]{1,0:T(8,128)S(1)} %get-tuple-element.11.fgrad_in), custom_call_target="tpu_custom_call" | custom-call | tf_op jit(solution)/shard_map/write_out/pallas_call | solution.py:515
